TPU v7x, 128 devices: a whole 4x4x4 slice. The times are simulated.
128 devices in a mesh: row: 16 (over x, z), col: 4 (over y_hi, core), tm: 2 (over y_lo).
Axes of the slice: x: 4, y: 4 (y_hi: 2, y_lo: 2; y = y_hi * 2 + y_lo), z: 4, core: 2. Of those that a mesh axis runs over, the one named last changes fastest.
Arguments:
- samples: bfloat16 [1024, 16, 2, 4096], P('row', None, 'tm', 'col'), may hold values from -6 to 6
- whitening: bfloat16 [1024, 1024], replicated, may hold values from -0.1875 to 0.1875
- ridge: float32 [2048], P('col'), may hold values from 2 to 20
- slab_start: int32 [1], replicated, may hold values from 0 to 63
- panels: int32 [4], replicated, may hold values from 0 to 3, as said below
Outputs:
- trailing: float32 [131072, 2048], P(('row', 'tm'), 'col')
- factor: bfloat16 [2, 131072, 512], P(None, ('row', 'tm'))
Inputs may be any that keep to these rules, and one draw needn't show every extreme that they name: `panels`: each panel index once.
All inputs are finite; a program needn't handle non-finite values.
Results may differ from a plain program's by a relative error of at most 0.012.
The roundings to bfloat16 on the way count: a program that leaves them out, or rounds other values in their place, can miss the bound.
Values may be sent and summed in bfloat16 or wider, within the bound.
No kernel may reach another device: no remote copies, remote signals or barrier semaphores. Data moves between devices by JAX's collectives and lax.ppermute only.
A program may use at most 192 MiB of HBM per device.

v0:
```python
import jax
import jax.numpy as jnp
from jax import lax
from jax.sharding import PartitionSpec as P

S = 1024
PANEL = 512
PANELS = 2


def broadcast(block, axis, holder):
    block = jnp.where(lax.axis_index(axis) == holder, block, jnp.zeros_like(block))
    return lax.psum(block, axis)


def rows_for(lines, devices):
    spare = -lines.shape[0] % devices
    if not spare:
        return lines
    return jnp.concatenate([lines, jnp.zeros((spare, *lines.shape[1:]), lines.dtype)])


def from_root(shard, axis, root):
    lines = jnp.where(lax.axis_index(axis) == root, shard, jnp.zeros_like(shard)).reshape(
        -1, *shard.shape[1:][-1:]
    )
    padded = rows_for(lines, lax.axis_size(axis))
    own = lax.psum_scatter(padded, axis, scatter_dimension=0, tiled=True)
    return lax.all_gather(own, axis, axis=0, tiled=True)[: len(lines)].reshape(shard.shape)


def broadcast_2(shard, axis, root):
    return lax.dynamic_index_in_dim(lax.all_gather(shard, axis), root, 0, keepdims=False)


def on_device(samples, whitening, ridge, slab_start, panels):
    moved = lax.all_to_all(samples, "row", split_axis=1, concat_axis=0, tiled=True)
    local_width = moved.shape[3]
    series = moved.reshape(moved.shape[0], local_width)
    whitened = jnp.dot(whitening, series, preferred_element_type=jnp.float32).astype(jnp.bfloat16)
    col_count = lax.axis_size("col")
    tm_count = lax.axis_size("tm")
    rows_here = col_count * local_width
    slab_width = PANEL * col_count
    scale = S ** (-0.5)
    slab_first = slab_start[0] * slab_width
    owner_index = slab_first // rows_here
    slab_offset = slab_first % rows_here
    col_index = lax.axis_index("col")
    self_index = lax.axis_index("row") * tm_count + lax.axis_index("tm")
    row_series = lax.all_gather(whitened, "col", axis=1, tiled=True)
    piece = lax.dynamic_slice_in_dim(row_series, slab_offset + col_index * PANEL, PANEL, 1)
    slab_part = broadcast(piece, ("row", "tm"), owner_index)
    covariance = (
        lax.dot_general(
            row_series, slab_part, (((0,), (0,)), ((), ())), preferred_element_type=jnp.float32
        )
        * scale
    )
    owner_flag = (self_index == owner_index).astype(jnp.float32)
    ridge_rows = slab_offset + col_index * PANEL
    zero_index = jnp.zeros((), jnp.int32)
    diag_block = (
        lax.dynamic_slice(covariance, (ridge_rows, zero_index), (PANEL, PANEL))
        + jnp.diag(ridge) * owner_flag
    )
    covariance = lax.dynamic_update_slice(covariance, diag_block, (ridge_rows, zero_index))
    identity = jnp.eye(PANEL, dtype=jnp.float32)
    factors = []
    finished = col_index < 0
    for section in range(PANELS):
        panel_index = panels[section]
        finished = finished | (col_index == panel_index)
        pivot_local = lax.dynamic_slice_in_dim(
            covariance, slab_offset + panel_index * PANEL, PANEL, 0
        )
        pivot_rows = from_root(pivot_local, ("row", "tm"), owner_index)
        pivot_safe = jnp.where(col_index == panel_index, pivot_rows, identity)
        lower_factor = jnp.linalg.cholesky(pivot_safe)
        panel_now = jax.scipy.linalg.solve_triangular(lower_factor, covariance.T, lower=True).T
        small_block = lower_factor
        panel_bf = broadcast_2(panel_now.astype(jnp.bfloat16), "col", panel_index)
        small_block = broadcast_2(small_block, "col", panel_index)
        coupling = jax.scipy.linalg.solve_triangular(small_block, pivot_rows, lower=True).T
        coupling_bf = coupling.astype(jnp.bfloat16)
        covariance = covariance - lax.dot_general(
            panel_bf, coupling_bf, (((1,), (1,)), ((), ())), preferred_element_type=jnp.float32
        )
        factors.append(panel_bf)
    trailing = jnp.where(finished, jnp.zeros_like(covariance), covariance)
    return (trailing, jnp.stack(factors))


def solution(mesh):
    in_specs = (P("row", None, "tm", "col"), P(), P("col"), P(), P())
    out_specs = (P(("row", "tm"), "col"), P(None, ("row", "tm"), None))
    return jax.shard_map(
        on_device, mesh=mesh, in_specs=in_specs, out_specs=out_specs, check_vma=False
    )
```

profile of v0, /device:TPU:1, one launch (start us, length us, event | category | flops | bytes accessed | tf_op | source)
XLA Modules:
  0.0 1696.4 jit_solution(11098721160999571711)
XLA Ops:
  10.1 34.7 %all_to_all.15 = bf16[64,16,1,1024]{3,0,2,1:T(8,128)(2,1)S(1)} all-to-all(bf16[64,16,1,1024]{3,0,2,1:T(8,128)(2,1)S(1)} %copy.24), channel_id=1, replica_groups=mesh['row'=16,'col'=4,'tm'=2] {'row'}, dimensions={1} | all-to-all | bytes 4194304 | tf_op jit(solution)/shard_map/all_to_all | solution.py:37
  44.8 3.7 convolution_convert_fusion
  49.3 62.6 %all-gather.12.cloned.1.call-done = bf16[1024,4096]{1,0:T(8,128)(2,1)} async-done(((bf16[1024,1024]{1,0:T(8,128)(2,1)}), bf16[1024,4096]{1,0:T(8,128)(2,1)}) %all-gather.12.cloned.1.call-update) | async-done | bytes 8388624 | tf_op jit(solution)/shard_map/all_gather | solution.py:51
  116.0 284.7 %all-reduce.3.cloned.1.call-done = bf16[1024,512]{1,0:T(8,128)(2,1)} async-done(((bf16[1024,512]{1,0:T(8,128)(2,1)}), bf16[1024,512]{1,0:T(8,128)(2,1)}) %all-reduce.3.cloned.1.call-update) | async-done | bytes 1048592 | tf_op jit(solution)/shard_map/psum | solution.py:13
  400.7 7.5 convolution_multiply_fusion
  412.0 5.8 dynamic_update_slice.3
  420.8 160.0 %reduce-scatter.7.cloned.1.call-done = f32[16,512]{1,0:T(8,128)} async-done(((f32[512,512]{1,0:T(8,128)}), f32[16,512]{1,0:T(8,128)}) %reduce-scatter.7.cloned.1.call-update) | async-done | bytes 32784 | tf_op jit(solution)/shard_map/reduce_scatter | solution.py:28
  581.7 149.1 %all-gather.14.cloned.1.call-done = f32[512,512]{1,0:T(8,128)} async-done(((f32[16,512]{1,0:T(8,128)}), f32[512,512]{1,0:T(8,128)}) %all-gather.14.cloned.1.call-update) | async-done | bytes 1048592 | tf_op jit(solution)/shard_map/all_gather | solution.py:29
  733.1 11.7 cholesky.286
  744.8 9.8 custom-call.31
  755.5 11.7 cholesky.305
  767.2 10.2 custom-call.32
  778.1 11.7 cholesky.326
  790.5 9.8 custom-call.33
  800.9 11.9 cholesky.343
  818.0 8.1 while.8
  826.0 39.3 %custom-call.34 = f32[4,128,128]{1,2,0:T(8,128)S(1)} custom-call(f32[4,128,128]{2,1,0:T(8,128)S(1)} %get-tuple-element.33), custom_call_target="InvertDiagBlocksLowerTriangular" | custom-call | tf_op jit(solution)/shard_map/jit(_solve_triangular)/triangular_solve | solution.py:80
  865.4 3.5 fusion.30
  868.9 3.5 convolution_subtract_fusion.4
  874.4 4.0 convolution_subtract_fusion.3
  880.4 5.9 fusion.15
  894.5 7.8 while.9
  902.4 39.3 %custom-call.35 = f32[4,128,128]{1,2,0:T(8,128)S(1)} custom-call(f32[4,128,128]{2,1,0:T(8,128)S(1)} %get-tuple-element.34), custom_call_target="InvertDiagBlocksLowerTriangular" | custom-call | tf_op jit(solution)/shard_map/jit(_solve_triangular)/triangular_solve | solution.py:84
  944.8 78.1 %all-gather.18.cloned.1.call-done = bf16[16384,512]{0,1:T(8,128)(2,1)} async-done(((bf16[4096,512]{0,1:T(8,128)(2,1)}), bf16[16384,512]{0,1:T(8,128)(2,1)}) %all-gather.18.cloned.1.call-update) | async-done | bytes 16777232 | tf_op jit(solution)/shard_map/all_gather | solution.py:33
  1022.9 22.4 %copy.40 = bf16[16384,512]{1,0:T(8,128)(2,1)} copy(bf16[16384,512]{0,1:T(8,128)(2,1)} %all-gather.18.cloned.1.call-done) | data formatting | bytes 33554432 | tf_op jit(solution)/shard_map/all_gather | solution.py:33
  1047.8 7.6 convolution_subtract_fusion
  1060.6 136.3 %reduce-scatter.9.cloned.1.call-done = f32[16,512]{1,0:T(8,128)} async-done(((f32[512,512]{1,0:T(8,128)}), f32[16,512]{1,0:T(8,128)}) %reduce-scatter.9.cloned.1.call-update) | async-done | bytes 32784 | tf_op jit(solution)/shard_map/reduce_scatter | solution.py:28
  1197.7 149.6 %all-gather.16.cloned.1.call-done = f32[512,512]{1,0:T(8,128)} async-done(((f32[16,512]{1,0:T(8,128)}), f32[512,512]{1,0:T(8,128)}) %all-gather.16.cloned.1.call-update) | async-done | bytes 1048592 | tf_op jit(solution)/shard_map/all_gather | solution.py:29
  1349.6 11.7 cholesky.358
  1362.0 9.8 custom-call.36
  1372.6 11.7 cholesky.377
  1385.1 10.2 custom-call.37
  1395.9 11.7 cholesky.398
  1408.3 9.8 custom-call.38
  1418.8 11.9 cholesky.415
  1435.1 7.7 while.10
  1442.8 39.3 %custom-call.39 = f32[4,128,128]{1,2,0:T(8,128)S(1)} custom-call(f32[4,128,128]{2,1,0:T(8,128)S(1)} %get-tuple-element.35), custom_call_target="InvertDiagBlocksLowerTriangular" | custom-call | tf_op jit(solution)/shard_map/jit(_solve_triangular)/triangular_solve | solution.py:80
  1482.1 3.5 fusion.28
  1485.6 3.5 convolution_subtract_fusion.2
  1491.1 4.0 convolution_subtract_fusion.1
  1497.1 5.7 fusion.12
  1510.5 8.3 while.11
  1518.8 39.3 %custom-call.40 = f32[4,128,128]{1,2,0:T(8,128)S(1)} custom-call(f32[4,128,128]{2,1,0:T(8,128)S(1)} %get-tuple-element.36), custom_call_target="InvertDiagBlocksLowerTriangular" | custom-call | tf_op jit(solution)/shard_map/jit(_solve_triangular)/triangular_solve | solution.py:84
  1561.3 78.4 %all-gather.22.cloned.1.call-done = bf16[16384,512]{0,1:T(8,128)(2,1)} async-done(((bf16[4096,512]{0,1:T(8,128)(2,1)}), bf16[16384,512]{0,1:T(8,128)(2,1)}) %all-gather.22.cloned.1.call-update) | async-done | bytes 16777232 | tf_op jit(solution)/shard_map/all_gather | solution.py:33
  1639.7 22.6 %copy.41 = bf16[16384,512]{1,0:T(8,128)(2,1)} copy(bf16[16384,512]{0,1:T(8,128)(2,1)} %all-gather.22.cloned.1.call-done) | data formatting | bytes 33554432 | tf_op jit(solution)/shard_map/all_gather | solution.py:33
  1664.8 6.4 pad_maximum_fusion
  1671.2 9.0 subtract_select_fusion
  1680.2 9.1 copy.36
  (173 shorter events, 96.9 us)
Async XLA Ops:
  7.2 37.7 %copy-start = (bf16[1024,1024]{1,0:T(8,128)(2,1)S(1)}, bf16[1024,1024]{1,0:T(8,128)(2,1)}, u32[]{:S(2)}) copy-start(bf16[1024,1024]{1,0:T(8,128)(2,1)} %param.11) | copy-start | bytes 6291460
  7.2 104.7 %all-gather.12.cloned.1.call-start = ((), (), s32[]{:S(2)}) async-start(), calls=%async_computation.3 | async-start | bytes 10485760 | tf_op jit(solution)/shard_map/all_gather | solution.py:51
  48.5 66.2 %copy-start.8 = (s32[4]{0:T(128)S(1)}, s32[4]{0:T(128)}, u32[]{:S(2)}) copy-start(s32[4]{0:T(128)} %param.14) | copy-start | bytes 52
  48.5 352.1 %all-reduce.3.cloned.1.call-start = ((), (), s32[]{:S(2)}) async-start(), calls=%async_computation.4 | async-start | bytes 2097152 | tf_op jit(solution)/shard_map/psum | solution.py:13
  114.7 466.1 %reduce-scatter.7.cloned.1.call-start = ((), (), s32[]{:S(2)}) async-start(), calls=%async_computation.11 | async-start | bytes 1081344 | tf_op jit(solution)/shard_map/reduce_scatter | solution.py:28
  116.0 295.6 %copy-start.7 = (f32[512]{0:T(512)S(1)}, f32[512]{0:T(512)}, u32[]{:S(2)}) copy-start(f32[512]{0:T(512)} %param.12) | copy-start | bytes 6148
  408.2 3.4 copy-start.3
  420.8 310.0 %all-gather.14.cloned.1.call-start = ((), (), s32[]{:S(2)}) async-start(), calls=%async_computation.5 | async-start | bytes 1081344 | tf_op jit(solution)/shard_map/all_gather | solution.py:29
  580.9 312.3 %all-gather.20.cloned.1.call-start = ((), (), s32[]{:S(2)}) async-start(), calls=%async_computation.8 | async-start | bytes 5242880 | tf_op jit(solution)/shard_map/all_gather | solution.py:33
  817.9 205.1 %all-gather.18.cloned.1.call-start = ((), (), s32[]{:S(2)}) async-start(), calls=%async_computation.7 | async-start | bytes 20971520 | tf_op jit(solution)/shard_map/all_gather | solution.py:33
  890.6 51.0 %copy-start.5 = (f32[512,512]{1,0:T(8,128)S(1)}, f32[512,512]{1,0:T(8,128)}, u32[]{:S(2)}) copy-start(f32[512,512]{1,0:T(8,128)} %all-gather.14.cloned.1.call-done) | copy-start | bytes 3145732
  890.7 306.2 %reduce-scatter.9.cloned.1.call-start = ((), (), s32[]{:S(2)}) async-start(), calls=%async_computation.12 | async-start | bytes 1081344 | tf_op jit(solution)/shard_map/reduce_scatter | solution.py:28
  1047.8 7.6 copy-start.4
  1055.4 3.4 copy-start.2
  1060.5 286.8 %all-gather.16.cloned.1.call-start = ((), (), s32[]{:S(2)}) async-start(), calls=%async_computation.6 | async-start | bytes 1081344 | tf_op jit(solution)/shard_map/all_gather | solution.py:29
  1196.9 312.3 %all-gather.24.cloned.1.call-start = ((), (), s32[]{:S(2)}) async-start(), calls=%async_computation.10 | async-start | bytes 5242880 | tf_op jit(solution)/shard_map/all_gather | solution.py:33
  1435.0 204.7 %all-gather.22.cloned.1.call-start = ((), (), s32[]{:S(2)}) async-start(), calls=%async_computation.9 | async-start | bytes 20971520 | tf_op jit(solution)/shard_map/all_gather | solution.py:33
  1507.1 51.0 %copy-start.6 = (f32[512,512]{1,0:T(8,128)S(1)}, f32[512,512]{1,0:T(8,128)}, u32[]{:S(2)}) copy-start(f32[512,512]{1,0:T(8,128)} %all-gather.16.cloned.1.call-done) | copy-start | bytes 3145732
  1680.2 9.1 copy-start.1
Sparse Core Ops, SparseCore 0:
  48.7 63.1 all-gather.11
  114.9 285.7 all-reduce.2
  420.9 159.9 reduce-scatter.6
  582.3 148.4 all-gather.13
  818.0 60.6 all-gather.19
  890.8 132.0 all-gather.17
  1060.6 136.1 reduce-scatter.8
  1198.6 148.7 all-gather.15
  1435.2 61.2 all-gather.23
  1507.3 132.3 all-gather.21
where the time goes:
time: 1700 us
  waiting for transfers between devices  1100 us (65%)
  other arithmetic  338 us (20%)
  local copies, waits for them, and re-layouts  113 us (7%)
  matrix products  83.3 us (5%)
  blocking collectives  34.7 us (2%)
  between operations  26.9 us (2%)
    all_gather x2, waiting for transfers between devices, from_root(): lax.all_gather(own, axis, axis=0, tiled=True)[:len(lines)]  299 us
    reduce_scatter x2, waiting for transfers between devices, from_root(): own = lax.psum_scatter(padded, axis, scatter_dimension=0, tiled=True)  296 us
    psum x1, waiting for transfers between devices, broadcast(): return lax.psum(block, axis)  285 us
    another operation x29, other arithmetic, on_device(): lower_factor = jnp.linalg.cholesky(pivot_safe)  158 us
    all_gather x4, waiting for transfers between devices, broadcast_2(): lax.all_gather(shard, axis)  157 us
    another operation x4, other arithmetic, on_device(): jax.scipy.linalg.solve_triangular(small_block, pivot_rows, lower=True)  81.3 us
    another operation x5, other arithmetic, on_device(): jax.scipy.linalg.solve_triangular(lower_factor, covariance.T, lower=True)  81.2 us
    all_gather x1, waiting for transfers between devices, on_device(): row_series = lax.all_gather(whitened, 'col', axis=1, tiled=True)  62.6 us
  transfers between devices with their start and end apart: 10, of which 8 were waited for; matrix products, arithmetic and copies ran while one was open for 15% of the time, Pallas kernels for 0%

commit v1 on v0

--- a/solution.py
+++ b/solution.py
@@ -10,7 +10,7 @@
 
 def broadcast(block, axis, holder):
     block = jnp.where(lax.axis_index(axis) == holder, block, jnp.zeros_like(block))
-    return lax.psum(block, axis)
+    return jnp.sum(lax.all_gather(block, axis), axis=0)
 
 
 def rows_for(lines, devices):

time: 1700 us -> 2120 us (1.25)
  waiting for transfers between devices: 1100 us -> 1500 us
    all_gather x0 -> x1, waiting for transfers between devices: none -> 706 us  [broadcast(): return jnp.sum(lax.all_gather(block, axis), axis=0)]
    psum x1 -> x0, waiting for transfers between devices: 285 us -> none  [broadcast(): return lax.psum(block, axis)]
  transfers between devices with their start and end apart: 10 -> 10, of which waited for: 8 -> 8; matrix products, arithmetic and copies ran while one was open for 15% -> 12% of each run, Pallas kernels for 0% -> 0%
where the time goes in v1:
time: 2120 us; the launch traced here: 2110 us
  waiting for transfers between devices  1500 us (71%)
  other arithmetic  350 us (17%)
  local copies, waits for them, and re-layouts  114 us (5%)
  matrix products  83 us (4%)
  blocking collectives  34.7 us (2%)
  between operations  27.8 us (1%)
    all_gather x1, waiting for transfers between devices, broadcast(): return jnp.sum(lax.all_gather(block, axis), axis=0)  706 us
    all_gather x2, waiting for transfers between devices, from_root(): lax.all_gather(own, axis, axis=0, tiled=True)[:len(lines)]  302 us
    reduce_scatter x2, waiting for transfers between devices, from_root(): own = lax.psum_scatter(padded, axis, scatter_dimension=0, tiled=True)  275 us
    another operation x29, other arithmetic, on_device(): lower_factor = jnp.linalg.cholesky(pivot_safe)  159 us
    all_gather x4, waiting for transfers between devices, broadcast_2(): lax.all_gather(shard, axis)  156 us
    another operation x4, other arithmetic, on_device(): jax.scipy.linalg.solve_triangular(small_block, pivot_rows, lower=True)  81.3 us
    another operation x5, other arithmetic, on_device(): jax.scipy.linalg.solve_triangular(lower_factor, covariance.T, lower=True)  81.2 us
    all_gather x1, waiting for transfers between devices, on_device(): row_series = lax.all_gather(whitened, 'col', axis=1, tiled=True)  62.6 us
  transfers between devices with their start and end apart: 10, of which 8 were waited for; matrix products, arithmetic and copies ran while one was open for 12% of the time, Pallas kernels for 0%

profile of v1, /device:TPU:1, one launch (start us, length us, event | category | flops | bytes accessed | tf_op | source)
XLA Modules:
  0.0 2112.3 jit_solution(8425039882487554838)
XLA Ops:
  10.1 34.7 %all_to_all.15 = bf16[64,16,1,1024]{3,0,2,1:T(8,128)(2,1)S(1)} all-to-all(bf16[64,16,1,1024]{3,0,2,1:T(8,128)(2,1)S(1)} %copy.24), channel_id=1, replica_groups=mesh['row'=16,'col'=4,'tm'=2] {'row'}, dimensions={1} | all-to-all | bytes 4194304 | tf_op jit(solution)/shard_map/all_to_all | solution.py:37
  44.8 3.7 convolution_convert_fusion
  49.3 62.6 %all-gather.14.cloned.1.call-done = bf16[1024,4096]{1,0:T(8,128)(2,1)} async-done(((bf16[1024,1024]{1,0:T(8,128)(2,1)}), bf16[1024,4096]{1,0:T(8,128)(2,1)}) %all-gather.14.cloned.1.call-update) | async-done | bytes 8388624 | tf_op jit(solution)/shard_map/all_gather | solution.py:51
  116.1 706.4 %all-gather.20.cloned.1.call-done = bf16[32768,512]{1,0:T(8,128)(2,1)} async-done(((bf16[1024,512]{1,0:T(8,128)(2,1)}), bf16[32768,512]{1,0:T(8,128)(2,1)}) %all-gather.20.cloned.1.call-update) | async-done | bytes 33554448 | tf_op jit(solution)/shard_map/all_gather | solution.py:13
  822.5 11.4 reduce_sum.12
  833.9 7.2 convolution_multiply_fusion
  844.9 5.8 dynamic_update_slice.3
  853.8 140.0 %reduce-scatter.7.cloned.1.call-done = f32[16,512]{1,0:T(8,128)} async-done(((f32[512,512]{1,0:T(8,128)}), f32[16,512]{1,0:T(8,128)}) %reduce-scatter.7.cloned.1.call-update) | async-done | bytes 32784 | tf_op jit(solution)/shard_map/reduce_scatter | solution.py:28
  994.8 150.7 %all-gather.16.cloned.1.call-done = f32[512,512]{1,0:T(8,128)} async-done(((f32[16,512]{1,0:T(8,128)}), f32[512,512]{1,0:T(8,128)}) %all-gather.16.cloned.1.call-update) | async-done | bytes 1048592 | tf_op jit(solution)/shard_map/all_gather | solution.py:29
  1147.7 11.7 cholesky.286
  1159.5 9.8 custom-call.31
  1170.1 11.7 cholesky.305
  1181.8 10.2 custom-call.32
  1192.8 11.7 cholesky.326
  1205.2 9.8 custom-call.33
  1215.6 11.9 cholesky.343
  1232.6 7.6 while.8
  1240.2 39.3 %custom-call.34 = f32[4,128,128]{1,2,0:T(8,128)S(1)} custom-call(f32[4,128,128]{2,1,0:T(8,128)S(1)} %get-tuple-element.33), custom_call_target="InvertDiagBlocksLowerTriangular" | custom-call | tf_op jit(solution)/shard_map/jit(_solve_triangular)/triangular_solve | solution.py:80
  1283.1 3.5 convolution_subtract_fusion.4
  1288.6 4.0 convolution_subtract_fusion.3
  1294.5 5.9 fusion.15
  1309.0 7.8 while.9
  1316.8 39.3 %custom-call.35 = f32[4,128,128]{1,2,0:T(8,128)S(1)} custom-call(f32[4,128,128]{2,1,0:T(8,128)S(1)} %get-tuple-element.34), custom_call_target="InvertDiagBlocksLowerTriangular" | custom-call | tf_op jit(solution)/shard_map/jit(_solve_triangular)/triangular_solve | solution.py:84
  1359.3 78.0 %all-gather.22.cloned.1.call-done = bf16[16384,512]{0,1:T(8,128)(2,1)} async-done(((bf16[4096,512]{0,1:T(8,128)(2,1)}), bf16[16384,512]{0,1:T(8,128)(2,1)}) %all-gather.22.cloned.1.call-update) | async-done | bytes 16777232 | tf_op jit(solution)/shard_map/all_gather | solution.py:33
  1437.4 22.4 %copy.40 = bf16[16384,512]{1,0:T(8,128)(2,1)} copy(bf16[16384,512]{0,1:T(8,128)(2,1)} %all-gather.22.cloned.1.call-done) | data formatting | bytes 33554432 | tf_op jit(solution)/shard_map/all_gather | solution.py:33
  1462.2 7.6 convolution_subtract_fusion
  1475.0 135.2 %reduce-scatter.9.cloned.1.call-done = f32[16,512]{1,0:T(8,128)} async-done(((f32[512,512]{1,0:T(8,128)}), f32[16,512]{1,0:T(8,128)}) %reduce-scatter.9.cloned.1.call-update) | async-done | bytes 32784 | tf_op jit(solution)/shard_map/reduce_scatter | solution.py:28
  1611.1 151.1 %all-gather.18.cloned.1.call-done = f32[512,512]{1,0:T(8,128)} async-done(((f32[16,512]{1,0:T(8,128)}), f32[512,512]{1,0:T(8,128)}) %all-gather.18.cloned.1.call-update) | async-done | bytes 1048592 | tf_op jit(solution)/shard_map/all_gather | solution.py:29
  1764.5 11.7 cholesky.358
  1776.9 9.8 custom-call.36
  1787.5 11.7 cholesky.377
  1799.9 10.2 custom-call.37
  1810.8 11.7 cholesky.398
  1823.2 9.8 custom-call.38
  1833.6 11.9 cholesky.415
  1850.2 8.3 while.10
  1858.5 39.3 %custom-call.39 = f32[4,128,128]{1,2,0:T(8,128)S(1)} custom-call(f32[4,128,128]{2,1,0:T(8,128)S(1)} %get-tuple-element.35), custom_call_target="InvertDiagBlocksLowerTriangular" | custom-call | tf_op jit(solution)/shard_map/jit(_solve_triangular)/triangular_solve | solution.py:80
  1897.8 3.5 fusion.28
  1901.3 3.6 convolution_subtract_fusion.2
  1906.9 4.0 convolution_subtract_fusion.1
  1912.9 5.7 fusion.12
  1926.3 8.3 while.11
  1934.6 39.3 %custom-call.40 = f32[4,128,128]{1,2,0:T(8,128)S(1)} custom-call(f32[4,128,128]{2,1,0:T(8,128)S(1)} %get-tuple-element.36), custom_call_target="InvertDiagBlocksLowerTriangular" | custom-call | tf_op jit(solution)/shard_map/jit(_solve_triangular)/triangular_solve | solution.py:84
  1977.1 78.3 %all-gather.26.cloned.1.call-done = bf16[16384,512]{0,1:T(8,128)(2,1)} async-done(((bf16[4096,512]{0,1:T(8,128)(2,1)}), bf16[16384,512]{0,1:T(8,128)(2,1)}) %all-gather.26.cloned.1.call-update) | async-done | bytes 16777232 | tf_op jit(solution)/shard_map/all_gather | solution.py:33
  2055.5 22.6 %copy.41 = bf16[16384,512]{1,0:T(8,128)(2,1)} copy(bf16[16384,512]{0,1:T(8,128)(2,1)} %all-gather.26.cloned.1.call-done) | data formatting | bytes 33554432 | tf_op jit(solution)/shard_map/all_gather | solution.py:33
  2080.6 6.4 pad_maximum_fusion
  2086.9 9.0 subtract_select_fusion
  2095.9 9.1 copy.36
  (174 shorter events, 100.6 us)
Async XLA Ops:
  7.2 37.7 %copy-start = (bf16[1024,1024]{1,0:T(8,128)(2,1)S(1)}, bf16[1024,1024]{1,0:T(8,128)(2,1)}, u32[]{:S(2)}) copy-start(bf16[1024,1024]{1,0:T(8,128)(2,1)} %param.11) | copy-start | bytes 6291460
  7.2 104.7 %all-gather.14.cloned.1.call-start = ((), (), s32[]{:S(2)}) async-start(), calls=%async_computation.3 | async-start | bytes 10485760 | tf_op jit(solution)/shard_map/all_gather | solution.py:51
  48.5 66.2 %copy-start.8 = (s32[4]{0:T(128)S(1)}, s32[4]{0:T(128)}, u32[]{:S(2)}) copy-start(s32[4]{0:T(128)} %param.14) | copy-start | bytes 52
  48.5 773.9 %all-gather.20.cloned.1.call-start = ((), (), s32[]{:S(2)}) async-start(), calls=%async_computation.6 | async-start | bytes 34603008 | tf_op jit(solution)/shard_map/all_gather | solution.py:13
  114.7 879.1 %reduce-scatter.7.cloned.1.call-start = ((), (), s32[]{:S(2)}) async-start(), calls=%async_computation.11 | async-start | bytes 1081344 | tf_op jit(solution)/shard_map/reduce_scatter | solution.py:28
  833.9 10.7 copy-start.7
  841.2 3.4 copy-start.3
  853.7 291.7 %all-gather.16.cloned.1.call-start = ((), (), s32[]{:S(2)}) async-start(), calls=%async_computation.4 | async-start | bytes 1081344 | tf_op jit(solution)/shard_map/all_gather | solution.py:29
  993.8 313.8 %all-gather.24.cloned.1.call-start = ((), (), s32[]{:S(2)}) async-start(), calls=%async_computation.8 | async-start | bytes 5242880 | tf_op jit(solution)/shard_map/all_gather | solution.py:33
  1232.5 204.8 %all-gather.22.cloned.1.call-start = ((), (), s32[]{:S(2)}) async-start(), calls=%async_computation.7 | async-start | bytes 20971520 | tf_op jit(solution)/shard_map/all_gather | solution.py:33
  1304.8 51.4 %copy-start.5 = (f32[512,512]{1,0:T(8,128)S(1)}, f32[512,512]{1,0:T(8,128)}, u32[]{:S(2)}) copy-start(f32[512,512]{1,0:T(8,128)} %all-gather.16.cloned.1.call-done) | copy-start | bytes 3145732
  1304.8 305.4 %reduce-scatter.9.cloned.1.call-start = ((), (), s32[]{:S(2)}) async-start(), calls=%async_computation.12 | async-start | bytes 1081344 | tf_op jit(solution)/shard_map/reduce_scatter | solution.py:28
  1462.2 7.6 copy-start.4
  1469.9 3.4 copy-start.2
  1475.0 287.2 %all-gather.18.cloned.1.call-start = ((), (), s32[]{:S(2)}) async-start(), calls=%async_computation.5 | async-start | bytes 1081344 | tf_op jit(solution)/shard_map/all_gather | solution.py:29
  1610.2 314.7 %all-gather.28.cloned.1.call-start = ((), (), s32[]{:S(2)}) async-start(), calls=%async_computation.10 | async-start | bytes 5242880 | tf_op jit(solution)/shard_map/all_gather | solution.py:33
  1850.2 205.3 %all-gather.26.cloned.1.call-start = ((), (), s32[]{:S(2)}) async-start(), calls=%async_computation.9 | async-start | bytes 20971520 | tf_op jit(solution)/shard_map/all_gather | solution.py:33
  1922.9 51.0 %copy-start.6 = (f32[512,512]{1,0:T(8,128)S(1)}, f32[512,512]{1,0:T(8,128)}, u32[]{:S(2)}) copy-start(f32[512,512]{1,0:T(8,128)} %all-gather.18.cloned.1.call-done) | copy-start | bytes 3145732
  2095.9 9.1 copy-start.1
Sparse Core Ops, SparseCore 0:
  48.7 63.1 all-gather.13
  114.8 707.6 all-gather.19
  853.8 139.9 reduce-scatter.6
  995.4 150.0 all-gather.15
  1232.7 61.1 all-gather.23
  1304.9 132.3 all-gather.21
  1475.1 135.0 reduce-scatter.8
  1611.8 150.3 all-gather.17
  1850.3 61.0 all-gather.27
  1923.1 132.3 all-gather.25
